TPU v7x, 128 devices: a whole 4x4x4 slice. The times are simulated.
128 devices in a mesh: kring: 8 (over y, x_lo), band: 16 (over z, x_hi, core).
Axes of the slice: x: 4 (x_hi: 2, x_lo: 2; x = x_hi * 2 + x_lo), y: 4, z: 4, core: 2. Of those that a mesh axis runs over, the one named last changes fastest.
Arguments:
- current: bfloat16 [262144, 256], P(('kring', 'band')), may hold values from -61 to 61
- previous: bfloat16 [262144, 256], P(('kring', 'band')), may hold values from -6 to 6
- energies: float32 [262144], P(('kring', 'band')), may hold values from 1.5 to 2.5
- targets: int32 [262144], P(('kring', 'band')), may hold values from 0 to 15, as said below
- layer_ids: int32 [327680], P(('kring', 'band')), may hold values from 0 to 1
- conduction_pairs: bfloat16 [327680, 1024], P(('kring', 'band')), may hold values from -0.375 to 0.375
- valence_pairs: bfloat16 [327680, 1024], P(('kring', 'band')), may hold values from -0.228125 to 0.228125
- exchange_pairs: bfloat16 [327680, 1024], P(('kring', 'band')), may hold values from -0.137001939 to 0.137001939
- screened: bfloat16 [8, 2, 1024, 2, 1024], P(None, None, 'band'), may hold values from -0.03203125 to 1.28203125
- coulomb: float32 [2, 2, 1024], replicated, may hold values from 0.2 to 2
- beta_prev: float32 [256], replicated, may hold values from 0.5 to 2
Outputs:
- next_vector: bfloat16 [262144, 256], P(('kring', 'band'))
- lanczos_alpha: float32 [256], replicated
- lanczos_beta: float32 [256], replicated
Inputs may be any that keep to these rules, and one draw needn't show every extreme that they name: `targets`: the 2048 rows of one device name each band index at most 2560 // 16 times; in every k-group one band index is named exactly that often by every device of the group.
All inputs are finite; a program needn't handle non-finite values.
Results may differ from a plain program's by a relative error of at most 0.0057.
Values may be sent and summed in bfloat16 or wider, within the bound.
A program may use at most 128 MiB of HBM per device.

v0:
```python
import jax
import jax.numpy as jnp
from jax import lax
from jax.sharding import PartitionSpec as P

epsilon_mean = 1e-06


def place_rows(targets, capacity, band_count):
    onehot = (targets[:, None] == jnp.arange(band_count, dtype=jnp.int32)[None, :]).astype(
        jnp.int32
    )
    counted = jnp.cumsum(onehot, axis=0)
    ranking = jnp.sum(counted * onehot, axis=1) - 1
    return targets * capacity + ranking


def per_device(
    current,
    previous,
    energies,
    targets,
    layer_ids,
    conduction_pairs,
    valence_pairs,
    exchange_pairs,
    screened,
    coulomb,
    beta_prev,
):
    band_count = lax.axis_size("band")
    own_rows, chains = current.shape
    slot_rows, basis_size = conduction_pairs.shape
    capacity = slot_rows // band_count
    slot_ids = place_rows(targets, capacity, band_count)
    outgoing = jnp.zeros((slot_rows, chains), jnp.bfloat16).at[slot_ids].set(current)
    arrived = lax.all_to_all(
        outgoing.reshape(band_count, capacity, chains),
        "band",
        split_axis=0,
        concat_axis=0,
        tiled=True,
    ).reshape(slot_rows, chains)
    layer_pick = (layer_ids[:, None] == jnp.arange(2, dtype=jnp.int32)[None, :]).astype(
        jnp.bfloat16
    )
    split_amps = arrived[:, None, :] * layer_pick[:, :, None]
    valence_part = jnp.einsum(
        "tg,tln->lgn", valence_pairs, split_amps, preferred_element_type=jnp.float32
    )
    exchange_part = jnp.einsum(
        "tg,tln->lgn", exchange_pairs, split_amps, preferred_element_type=jnp.float32
    )
    projected = lax.psum_scatter(valence_part, "band", scatter_dimension=1, tiled=True).astype(
        jnp.bfloat16
    )
    exchange_total = lax.psum(exchange_part, ("kring", "band"))
    coupled = (
        coulomb[:, 0, :, None] * exchange_total[0][None]
        + coulomb[:, 1, :, None] * exchange_total[1][None]
    ).astype(jnp.bfloat16)
    group_index = lax.axis_index("kring")
    group_count = lax.axis_size("kring")
    pieces = lax.all_gather(projected[None], "kring", axis=0, tiled=True)
    number = pieces.shape[0]
    distance = jnp.mod(group_index - jnp.arange(number, dtype=jnp.int32), group_count)
    blocks = jnp.take(screened, distance, axis=0)
    direct_part = jnp.einsum("kaphg,kapn->hgn", blocks, pieces, preferred_element_type=jnp.float32)
    direct = lax.psum(direct_part, "band").astype(jnp.bfloat16)
    both_direct = jnp.einsum(
        "tg,lgn->tln", conduction_pairs, direct, preferred_element_type=jnp.float32
    )
    both_exchange = jnp.einsum(
        "tg,lgn->tln", exchange_pairs, coupled, preferred_element_type=jnp.float32
    )
    kernel_all = 2.0 * both_exchange - both_direct
    kernel_rows = jnp.sum(kernel_all * layer_pick.astype(jnp.float32)[:, :, None], axis=1).astype(
        jnp.bfloat16
    )
    returned = lax.all_to_all(
        kernel_rows.reshape(band_count, capacity, chains),
        "band",
        split_axis=0,
        concat_axis=0,
        tiled=True,
    ).reshape(slot_rows, chains)
    kernel_own = returned[slot_ids].astype(jnp.float32)
    current_wide = current.astype(jnp.float32)
    applied = energies[:, None] * current_wide + kernel_own
    start_vec = applied - beta_prev[None, :] * previous.astype(jnp.float32)
    total_rows = own_rows * group_count * band_count
    projection, self_norm = lax.psum(
        (jnp.sum(current_wide * start_vec, axis=0), jnp.sum(current_wide * current_wide, axis=0)),
        ("kring", "band"),
    )
    lanczos_alpha = projection / self_norm
    residual = start_vec - lanczos_alpha[None, :] * current_wide
    residual_sq = lax.psum(jnp.sum(residual * residual, axis=0), ("kring", "band"))
    lanczos_beta = jnp.sqrt(residual_sq / total_rows + epsilon_mean)
    next_vector = (residual / lanczos_beta[None, :]).astype(jnp.bfloat16)
    return (next_vector, lanczos_alpha, lanczos_beta)


def solution(mesh):
    in_specs = (
        P(("kring", "band"), None),
        P(("kring", "band"), None),
        P(("kring", "band")),
        P(("kring", "band")),
        P(("kring", "band")),
        P(("kring", "band"), None),
        P(("kring", "band"), None),
        P(("kring", "band"), None),
        P(None, None, "band", None, None),
        P(),
        P(),
    )
    out_specs = (P(("kring", "band"), None), P(), P())
    return jax.shard_map(
        per_device, mesh=mesh, in_specs=in_specs, out_specs=out_specs, check_vma=False
    )
```

profile of v0, /device:TPU:1, one launch (start us, length us, event | category | flops | bytes accessed | tf_op | source)
XLA Modules:
  0.0 529.2 jit_solution(18126593749929816699)
XLA Ops:
  7.2 0.7 fusion.48
  7.9 4.5 reduce-window.6
  12.4 0.4 slice_reduce_fusion
  13.2 0.8 fusion.47
  13.9 0.7 broadcast_clamp_fusion
  14.7 10.8 %scatter_custom_fusion = bf16[2560,256]{1,0:T(8,128)(2,1)} fusion(s32[2048]{0:T(1024)S(1)} %get-tuple-element.8, bf16[2048,256]{1,0:T(8,128)(2,1)} %param.11, bf16[]{:T(256)} %constant.46.clone.1), kind=kCustom, calls=%fused_computation.44 | custom fusion | bytes 1311232 | tf_op jit(solution)/shard_map/scatter | solution.py:36
  25.5 9.3 %all-to-all-start = ((bf16[16,160,256]{2,1,0:T(8,128)(2,1)}), bf16[16,160,256]{2,1,0:T(8,128)(2,1)S(1)}, u32[]{:S(2)}, u32[]{:S(2)}) async-start(bf16[16,160,256]{2,1,0:T(8,128)(2,1)} %bitcast.2), calls=%async_computation | async-start | bytes 2621440 | tf_op jit(solution)/shard_map/all_to_all | solution.py:37
  34.8 0.2 all-reduce.6.cloned.1.call-start
  35.1 0.6 dynamic-slice
  36.4 12.0 %gather_fusion = bf16[8,2,64,2,1024]{4,3,2,1,0:T(2,128)(2,1)} fusion(bf16[8,2,64,2,1024]{4,3,2,1,0:T(2,128)(2,1)} %param.19, s32[1024]{0:T(1024)S(1)} %pad_clamp_fusion), kind=kCustom, calls=%fused_computation | custom fusion | bytes 8388640 | tf_op jit(solution)/shard_map/jit(_take)/gather | solution.py:67
  48.4 7.8 %broadcast_select_fusion = bf16[8,2,64,2,1024]{4,3,2,1,0:T(2,128)(2,1)} fusion(bf16[8,2,64,2,1024]{4,3,2,1,0:T(2,128)(2,1)} %gather_fusion, pred[8]{0:T(512)(128)(4,1)S(1)} %compare_and_fusion), kind=kLoop, calls=%fused_computation.3 | loop fusion | flops 2097152 | bytes 8388616 | tf_op jit(solution)/shard_map/jit(_take)/select_n | solution.py:67
  56.2 0.8 copy.21
  57.0 6.7 %fusion.28 = f32[2,1024,256]{1,2,0:T(8,128)} fusion(bf16[2560,1024]{1,0:T(8,128)(2,1)} %param.17, bf16[2560,2]{0,1:T(2,128)(2,1)S(1)} %get-tuple-element.10, bf16[2560,256]{0,1:T(8,128)(2,1)S(1)} %copy.21), kind=kOutput, calls=%fused_computation.32 | convolution fusion | flops 2685665280 | bytes 8660992 | tf_op jit(solution)/shard_map/tg,tln->lgn/dot_general | solution.py:48
  63.6 2.8 copy.22
  66.5 84.6 %all-reduce.7 = bf16[2,1024,256]{2,0,1:T(2,128)(2,1)} all-reduce(f32[2,1024,256]{2,0,1:T(2,128)S(1)} %copy.22), channel_id=3, replica_groups=mesh['kring'=8,'band'=16] {'band'}, use_global_device_ids=true, to_apply=%region_5.6.clone | all-reduce | flops 524288 | bytes 3145728
  151.1 0.9 dynamic-slice_convert_fusion
  152.0 25.1 %all-gather = bf16[16,64,256]{2,1,0:T(8,128)(2,1)S(1)} all-gather(bf16[2,64,256]{2,1,0:T(8,128)(2,1)S(1)} %copy.23), channel_id=2, replica_groups=mesh['kring'=8,'band'=16] {'kring'}, dimensions={0}, use_global_device_ids=true | all-gather | bytes 589824 | tf_op jit(solution)/shard_map/all_gather | solution.py:64
  177.1 4.3 fusion.20
  181.4 4.3 fusion.23
  185.7 91.2 %all-reduce.8 = bf16[2,1024,256]{2,1,0:T(8,128)(2,1)S(1)} all-reduce(f32[2,1024,256]{2,1,0:T(8,128)S(1)} %fusion.20), channel_id=1, replica_groups=mesh['kring'=8,'band'=16] {'band'}, use_global_device_ids=true, to_apply=%region_6.7 | all-reduce | flops 524288 | bytes 3145728 | tf_op jit(solution)/shard_map/psum | solution.py:69
  277.0 7.3 %fusion.1 = f32[2,256,2560]{2,1,0:T(8,128)} fusion(bf16[2560,1024]{1,0:T(8,128)(2,1)} %param.16, bf16[2,1024,256]{2,1,0:T(8,128)(2,1)S(1)} %all-reduce.8), kind=kOutput, calls=%fused_computation.6 | convolution fusion | flops 2684354560 | bytes 11534336 | tf_op jit(solution)/shard_map/tg,lgn->tln/dot_general | solution.py:70
  284.3 64.9 %all-reduce.6.cloned.1.call-done = f32[2,1024,256]{1,2,0:T(8,128)} async-done(((f32[2,1024,256]{1,2,0:T(8,128)}), f32[2,1024,256]{1,2,0:T(8,128)}) %all-reduce.6.cloned.1.call-update) | async-done | bytes 2097168 | tf_op jit(solution)/shard_map/psum | solution.py:57
  349.2 1.7 slice_bitcast_fusion.1
  350.9 6.9 %fusion = bf16[2560,256]{0,1:T(8,128)(2,1)S(1)} fusion(f32[2,256,2560]{2,1,0:T(8,128)} %fusion.1, bf16[2560,1024]{1,0:T(8,128)(2,1)} %param.18, f32[2560,2]{0,1:T(2,128)S(1)} %get-tuple-element.9, f32[1024,256]{0,1:T(8,128)S(1)} %get-tuple-element.12, f32[2,1024]{1,0:T(2,128)S(1)} %get-tuple-element.15, f32[1024,256]{0,1:T(8,128)S(1)} %get-tuple-element.11, ...), kind=kOutput, calls=%fused_computation.5 | convolution fusion | flops 2691039232 | bytes 13930496 | tf_op jit(solution)/shard_map/tg,lgn->tln/dot_general | solution.py:73
  357.8 0.6 copy.27
  358.4 25.4 %all_to_all.10 = bf16[16,160,256]{2,1,0:T(8,128)(2,1)S(1)} all-to-all(bf16[16,160,256]{2,1,0:T(8,128)(2,1)S(1)} %bitcast.66), channel_id=1, replica_groups=mesh['kring'=8,'band'=16] {'band'}, dimensions={0} | all-to-all | bytes 2621440 | tf_op jit(solution)/shard_map/all_to_all | solution.py:80
  383.8 7.5 %gather_fusion.1 = bf16[2048,256]{1,0:T(8,128)(2,1)S(1)} fusion(bf16[2560,256]{1,0:T(8,128)(2,1)S(1)} %bitcast.64, s32[2048]{0:T(1024)S(1)} %get-tuple-element.7), kind=kCustom, calls=%fused_computation.1 | custom fusion | bytes 2105344 | tf_op jit(solution)/shard_map/gather | solution.py:87
  391.4 2.1 fusion.18
  393.5 63.6 %all-reduce.1 = (f32[256]{0:T(256)S(1)}, f32[256]{0:T(256)S(1)}) all-reduce(f32[256]{0:T(256)S(1)} %get-tuple-element.4, f32[256]{0:T(256)S(1)} %get-tuple-element.3), channel_id=1, replica_groups=mesh['kring'=8,'band'=16] {'kring','band'}, use_global_device_ids=true, to_apply=%region_9.10 | all-reduce | flops 512 | bytes 4096 | tf_op jit(solution)/shard_map/psum | solution.py:92
  457.1 0.8 multiply_reduce_fusion
  457.9 62.7 %psum.39 = f32[256]{0:T(256)S(1)} all-reduce(f32[256]{0:T(256)S(1)} %multiply_reduce_fusion), channel_id=1, replica_groups=mesh['kring'=8,'band'=16] {'kring','band'}, use_global_device_ids=true, to_apply=%region_13.14 | all-reduce | flops 256 | bytes 2048 | tf_op jit(solution)/shard_map/psum | solution.py:98
  520.6 1.7 divide_convert_fusion
  (36 shorter events, 0.4 us)
Async XLA Ops:
  13.1 21.9 %copy-start.4 = (s32[2560]{0:T(1024)S(1)}, s32[2560]{0:T(1024)}, u32[]{:S(2)}) copy-start(s32[2560]{0:T(1024)} %param.15) | copy-start | bytes 30724
  13.2 21.9 %copy-start.3 = (f32[2,2,1024]{2,1,0:T(2,128)S(1)}, f32[2,2,1024]{2,1,0:T(2,128)}, u32[]{:S(2)}) copy-start(f32[2,2,1024]{2,1,0:T(2,128)} %param.20) | copy-start | bytes 49156
  13.2 22.0 %copy-start.8 = (u32[128]{0:T(128)S(1)}, u32[128]{0:T(128)}, u32[]{:S(2)}) copy-start(u32[128]{0:T(128)} %constant.62) | copy-start | bytes 1540
  25.5 30.7 %all-to-all-start = ((bf16[16,160,256]{2,1,0:T(8,128)(2,1)}), bf16[16,160,256]{2,1,0:T(8,128)(2,1)S(1)}, u32[]{:S(2)}, u32[]{:S(2)}) async-start(bf16[16,160,256]{2,1,0:T(8,128)(2,1)} %bitcast.2), calls=%async_computation | async-start | bytes 2621440 | tf_op jit(solution)/shard_map/all_to_all | solution.py:37
  34.8 314.4 %all-reduce.6.cloned.1.call-start = ((), (), s32[]{:S(2)}) async-start(), calls=%async_computation.2 | async-start | bytes 4194304 | tf_op jit(solution)/shard_map/psum | solution.py:57
  152.0 29.4 %slice-start = ((s8[5242880]{0:T(1024)(128)(4,1)}), s8[4194304]{0:T(1024)(128)(4,1)S(1)}, s32[]{:S(2)}) async-start(s8[5242880]{0:T(1024)(128)(4,1)} %bitcast.71), calls=%async_computation.3 | async-start | bytes 8388608
  177.1 4.3 slice-start.1
  383.8 7.5 %copy-start = (bf16[2048,256]{1,0:T(8,128)(2,1)S(1)}, bf16[2048,256]{1,0:T(8,128)(2,1)}, u32[]{:S(2)}) copy-start(bf16[2048,256]{1,0:T(8,128)(2,1)} %param.11) | copy-start | bytes 3145732
  383.8 7.5 %copy-start.2 = (f32[2048]{0:T(1024)S(1)}, f32[2048]{0:T(1024)}, u32[]{:S(2)}) copy-start(f32[2048]{0:T(1024)} %param.13) | copy-start | bytes 24580
  383.8 7.5 %copy-start.5 = (f32[256]{0:T(256)S(1)}, f32[256]{0:T(256)}, u32[]{:S(2)}) copy-start(f32[256]{0:T(256)} %param.21) | copy-start | bytes 3076
  391.4 65.7 %copy-start.1 = (bf16[2048,256]{1,0:T(8,128)(2,1)S(1)}, bf16[2048,256]{1,0:T(8,128)(2,1)}, u32[]{:S(2)}) copy-start(bf16[2048,256]{1,0:T(8,128)(2,1)} %param.12) | copy-start | bytes 3145732
  457.1 65.3 %copy-start.6 = (f32[256]{0:T(256)}, f32[256]{0:T(256)S(1)}, u32[]{:S(2)}) copy-start(f32[256]{0:T(256)S(1)} %div.17) | copy-start | bytes 3076
  520.6 1.8 copy-start.7
Sparse Core Ops, SparseCore 0:
  185.9 163.2 all-reduce.5
where the time goes:
time: 530 us; the launch traced here: 529 us
  blocking collectives  353 us (67%)
  waiting for transfers between devices  64.9 us (12%)
  local copies, waits for them, and re-layouts  38.2 us (7%)
  matrix products  29.5 us (6%)
  other arithmetic  19.5 us (4%)
  between operations  14.9 us (3%)
  starting transfers between devices  9.51 us (2%)
    psum x1, blocking collectives, per_device(): direct = lax.psum(direct_part, 'band').astype(jnp.bfloat16)  91.2 us
    unnamed x1, blocking collectives  84.6 us
    psum x1, waiting for transfers between devices, per_device(): exchange_total = lax.psum(exchange_part, ('kring', 'band'))  64.9 us
    psum x1, blocking collectives, per_device(): lax.psum((jnp.sum(current_wide * start_vec, axis=0), jnp.sum(current_wide...  63.6 us
    psum x1, blocking collectives, per_device(): lax.psum(jnp.sum(residual * residual, axis=0), ('kring', 'band'))  62.7 us
    all_to_all x1, blocking collectives, per_device(): lax.all_to_all(kernel_rows.reshape(band_count, capacity, chains), 'band',...  25.4 us
    all_gather x1, blocking collectives, per_device(): pieces = lax.all_gather(projected[None], 'kring', axis=0, tiled=True)  25.1 us
    gather x1, local copies, waits for them, and re-layouts, per_device(): blocks = jnp.take(screened, distance, axis=0)  12 us
  transfers between devices with their start and end apart: 2, of which 1 were waited for; matrix products, arithmetic and copies ran while one was open for 5% of the time, Pallas kernels for 0%

commit v1 on v0

--- a/solution.py
+++ b/solution.py
@@ -61,7 +61,9 @@
     ).astype(jnp.bfloat16)
     group_index = lax.axis_index("kring")
     group_count = lax.axis_size("kring")
-    pieces = lax.all_gather(projected[None], "kring", axis=0, tiled=True)
+    pieces = jnp.concatenate(
+        lax.all_to_all(jnp.stack([projected[None]] * lax.axis_size("kring")), "kring", 0, 0), axis=0
+    )
     number = pieces.shape[0]
     distance = jnp.mod(group_index - jnp.arange(number, dtype=jnp.int32), group_count)
     blocks = jnp.take(screened, distance, axis=0)

time: 530 us -> 506 us (0.955)
  blocking collectives: 353 us -> 324 us
    all_gather x1 -> x0, blocking collectives: 25.1 us -> none  [per_device(): pieces = lax.all_gather(projected[None], 'kring', axis=0, tiled=True)]
  transfers between devices with their start and end apart: 2 -> 3, of which waited for: 1 -> 2; matrix products, arithmetic and copies ran while one was open for 5% -> 8% of each run, Pallas kernels for 0% -> 0%
where the time goes in v1:
time: 506 us; the launch traced here: 505 us
  blocking collectives  324 us (64%)
  waiting for transfers between devices  62.1 us (12%)
  local copies, waits for them, and re-layouts  39.1 us (8%)
  matrix products  31.9 us (6%)
  other arithmetic  19.5 us (4%)
  between operations  14.9 us (3%)
  starting transfers between devices  13.8 us (3%)
    psum x1, blocking collectives, per_device(): direct = lax.psum(direct_part, 'band').astype(jnp.bfloat16)  87.9 us
    unnamed x1, blocking collectives  84.6 us
    psum x1, blocking collectives, per_device(): lax.psum((jnp.sum(current_wide * start_vec, axis=0), jnp.sum(current_wide...  63.6 us
    psum x1, blocking collectives, per_device(): lax.psum(jnp.sum(residual * residual, axis=0), ('kring', 'band'))  62.7 us
    psum x1, waiting for transfers between devices, per_device(): exchange_total = lax.psum(exchange_part, ('kring', 'band'))  61.4 us
    all_to_all x1, blocking collectives, per_device(): lax.all_to_all(kernel_rows.reshape(band_count, capacity, chains), 'band',...  25.4 us
    gather x1, local copies, waits for them, and re-layouts, per_device(): blocks = jnp.take(screened, distance, axis=0)  12 us
    scatter x1, local copies, waits for them, and re-layouts, per_device(): jnp.zeros((slot_rows, chains), jnp.bfloat16).at[slot_ids].set(current)  10.8 us
  transfers between devices with their start and end apart: 3, of which 2 were waited for; matrix products, arithmetic and copies ran while one was open for 8% of the time, Pallas kernels for 0%

profile of v1, /device:TPU:1, one launch (start us, length us, event | category | flops | bytes accessed | tf_op | source)
XLA Modules:
  0.0 505.4 jit_solution(2525513769986910684)
XLA Ops:
  7.2 0.7 fusion.48
  7.9 4.5 reduce-window.6
  13.2 0.8 fusion.47
  13.9 0.7 broadcast_clamp_fusion
  14.7 10.8 %scatter_custom_fusion = bf16[2560,256]{1,0:T(8,128)(2,1)} fusion(s32[2048]{0:T(1024)S(1)} %get-tuple-element.8, bf16[2048,256]{1,0:T(8,128)(2,1)} %param.11, bf16[]{:T(256)} %constant.46.clone.1), kind=kCustom, calls=%fused_computation.44 | custom fusion | bytes 1311232 | tf_op jit(solution)/shard_map/scatter | solution.py:36
  25.5 9.3 %all-to-all-start = ((bf16[16,160,256]{2,1,0:T(8,128)(2,1)}), bf16[16,160,256]{2,1,0:T(8,128)(2,1)S(1)}, u32[]{:S(2)}, u32[]{:S(2)}) async-start(bf16[16,160,256]{2,1,0:T(8,128)(2,1)} %bitcast.2), calls=%async_computation | async-start | bytes 2621440 | tf_op jit(solution)/shard_map/all_to_all | solution.py:37
  34.9 0.6 dynamic-slice
  36.1 12.0 %gather_fusion = bf16[8,2,64,2,1024]{4,3,2,1,0:T(2,128)(2,1)} fusion(bf16[8,2,64,2,1024]{4,3,2,1,0:T(2,128)(2,1)} %param.19, s32[1024]{0:T(1024)S(1)} %pad_clamp_fusion), kind=kCustom, calls=%fused_computation | custom fusion | bytes 8388640 | tf_op jit(solution)/shard_map/jit(_take)/gather | solution.py:69
  48.2 7.8 %broadcast_select_fusion = bf16[8,2,64,2,1024]{4,3,2,1,0:T(2,128)(2,1)} fusion(bf16[8,2,64,2,1024]{4,3,2,1,0:T(2,128)(2,1)} %gather_fusion, pred[8]{0:T(512)(128)(4,1)S(1)} %compare_and_fusion), kind=kLoop, calls=%fused_computation.3 | loop fusion | flops 2097152 | bytes 8388616 | tf_op jit(solution)/shard_map/jit(_take)/select_n | solution.py:69
  56.0 0.8 copy.29
  56.7 6.7 %fusion.28 = f32[2,1024,256]{1,2,0:T(8,128)} fusion(bf16[2560,1024]{1,0:T(8,128)(2,1)} %param.17, bf16[2560,2]{0,1:T(2,128)(2,1)S(1)} %get-tuple-element.10, bf16[2560,256]{0,1:T(8,128)(2,1)S(1)} %copy.29), kind=kOutput, calls=%fused_computation.32 | convolution fusion | flops 2685665280 | bytes 8660992 | tf_op jit(solution)/shard_map/tg,tln->lgn/dot_general | solution.py:48
  63.4 2.8 copy.30
  66.3 84.6 %all-reduce.7 = bf16[2,1024,256]{2,0,1:T(2,128)(2,1)} all-reduce(f32[2,1024,256]{2,0,1:T(2,128)S(1)} %copy.30), channel_id=2, replica_groups=mesh['kring'=8,'band'=16] {'band'}, use_global_device_ids=true, to_apply=%region_5.6.clone | all-reduce | flops 524288 | bytes 3145728
  150.8 0.9 dynamic-slice_convert_fusion
  151.7 0.8 stack.3
  152.6 4.2 all-to-all-start.1
  157.1 6.7 %fusion.23 = f32[2,1024,256]{1,2,0:T(8,128)} fusion(bf16[2560,1024]{1,0:T(8,128)(2,1)} %param.18, bf16[2560,2]{0,1:T(2,128)(2,1)S(1)} %get-tuple-element.10, bf16[2560,256]{0,1:T(8,128)(2,1)S(1)} %copy.29), kind=kOutput, calls=%fused_computation.31 | convolution fusion | flops 2685665280 | bytes 8660992 | tf_op jit(solution)/shard_map/tg,tln->lgn/dot_general | solution.py:51
  163.8 0.6 all-to-all-done.1
  164.4 4.3 fusion.20
  168.8 87.9 %all-reduce.8 = bf16[2,1024,256]{2,1,0:T(8,128)(2,1)S(1)} all-reduce(f32[2,1024,256]{2,1,0:T(8,128)S(1)} %fusion.20), channel_id=1, replica_groups=mesh['kring'=8,'band'=16] {'band'}, use_global_device_ids=true, to_apply=%region_6.7 | all-reduce | flops 524288 | bytes 3145728 | tf_op jit(solution)/shard_map/psum | solution.py:71
  256.6 7.3 %fusion.1 = f32[2,256,2560]{2,1,0:T(8,128)} fusion(bf16[2560,1024]{1,0:T(8,128)(2,1)} %param.16, bf16[2,1024,256]{2,1,0:T(8,128)(2,1)S(1)} %all-reduce.8), kind=kOutput, calls=%fused_computation.6 | convolution fusion | flops 2684354560 | bytes 11534336 | tf_op jit(solution)/shard_map/tg,lgn->tln/dot_general | solution.py:72
  264.0 61.4 %all-reduce.6.cloned.1.call-done = f32[2,1024,256]{1,2,0:T(8,128)} async-done(((f32[2,1024,256]{1,2,0:T(8,128)}), f32[2,1024,256]{1,2,0:T(8,128)}) %all-reduce.6.cloned.1.call-update) | async-done | bytes 2097168 | tf_op jit(solution)/shard_map/psum | solution.py:57
  325.4 1.7 slice_bitcast_fusion.1
  327.1 6.9 %fusion = bf16[2560,256]{0,1:T(8,128)(2,1)S(1)} fusion(f32[2,256,2560]{2,1,0:T(8,128)} %fusion.1, bf16[2560,1024]{1,0:T(8,128)(2,1)} %param.18, f32[2560,2]{0,1:T(2,128)S(1)} %get-tuple-element.9, f32[1024,256]{0,1:T(8,128)S(1)} %get-tuple-element.12, f32[2,1024]{1,0:T(2,128)S(1)} %get-tuple-element.15, f32[1024,256]{0,1:T(8,128)S(1)} %get-tuple-element.11, ...), kind=kOutput, calls=%fused_computation.5 | convolution fusion | flops 2691039232 | bytes 13930496 | tf_op jit(solution)/shard_map/tg,lgn->tln/dot_general | solution.py:75
  334.0 0.6 copy.35
  334.6 25.4 %all_to_all.15 = bf16[16,160,256]{2,1,0:T(8,128)(2,1)S(1)} all-to-all(bf16[16,160,256]{2,1,0:T(8,128)(2,1)S(1)} %bitcast.66), channel_id=1, replica_groups=mesh['kring'=8,'band'=16] {'band'}, dimensions={0} | all-to-all | bytes 2621440 | tf_op jit(solution)/shard_map/all_to_all | solution.py:82
  360.0 7.5 %gather_fusion.1 = bf16[2048,256]{1,0:T(8,128)(2,1)S(1)} fusion(bf16[2560,256]{1,0:T(8,128)(2,1)S(1)} %bitcast.64, s32[2048]{0:T(1024)S(1)} %get-tuple-element.7), kind=kCustom, calls=%fused_computation.1 | custom fusion | bytes 2105344 | tf_op jit(solution)/shard_map/gather | solution.py:89
  367.6 2.1 fusion.18
  369.7 63.6 %all-reduce.1 = (f32[256]{0:T(256)S(1)}, f32[256]{0:T(256)S(1)}) all-reduce(f32[256]{0:T(256)S(1)} %get-tuple-element.4, f32[256]{0:T(256)S(1)} %get-tuple-element.3), channel_id=1, replica_groups=mesh['kring'=8,'band'=16] {'kring','band'}, use_global_device_ids=true, to_apply=%region_9.10 | all-reduce | flops 512 | bytes 4096 | tf_op jit(solution)/shard_map/psum | solution.py:94
  433.3 0.8 multiply_reduce_fusion
  434.1 62.7 %psum.39 = f32[256]{0:T(256)S(1)} all-reduce(f32[256]{0:T(256)S(1)} %multiply_reduce_fusion), channel_id=1, replica_groups=mesh['kring'=8,'band'=16] {'kring','band'}, use_global_device_ids=true, to_apply=%region_13.14 | all-reduce | flops 256 | bytes 2048 | tf_op jit(solution)/shard_map/psum | solution.py:100
  496.8 1.7 divide_convert_fusion
  (33 shorter events, 1.1 us)
Async XLA Ops:
  13.1 21.7 %copy-start.4 = (s32[2560]{0:T(1024)S(1)}, s32[2560]{0:T(1024)}, u32[]{:S(2)}) copy-start(s32[2560]{0:T(1024)} %param.15) | copy-start | bytes 30724
  13.2 21.7 %copy-start.3 = (f32[2,2,1024]{2,1,0:T(2,128)S(1)}, f32[2,2,1024]{2,1,0:T(2,128)}, u32[]{:S(2)}) copy-start(f32[2,2,1024]{2,1,0:T(2,128)} %param.20) | copy-start | bytes 49156
  13.2 21.7 %copy-start.8 = (u32[128]{0:T(128)S(1)}, u32[128]{0:T(128)}, u32[]{:S(2)}) copy-start(u32[128]{0:T(128)} %constant.62) | copy-start | bytes 1540
  25.5 30.5 %all-to-all-start = ((bf16[16,160,256]{2,1,0:T(8,128)(2,1)}), bf16[16,160,256]{2,1,0:T(8,128)(2,1)S(1)}, u32[]{:S(2)}, u32[]{:S(2)}) async-start(bf16[16,160,256]{2,1,0:T(8,128)(2,1)} %bitcast.2), calls=%async_computation | async-start | bytes 2621440 | tf_op jit(solution)/shard_map/all_to_all | solution.py:37
  152.6 11.9 %all-to-all-start.1 = ((bf16[8,1,2,64,256]{4,3,2,1,0:T(8,128)(2,1)}), bf16[8,1,2,64,256]{4,3,2,1,0:T(8,128)(2,1)}, u32[]{:S(2)}, u32[]{:S(2)}) async-start(bf16[8,1,2,64,256]{4,3,2,1,0:T(8,128)(2,1)} %stack.3), calls=%async_computation.1 | async-start | bytes 1048576 | tf_op jit(solution)/shard_map/all_to_all | solution.py:65
  156.8 168.6 %all-reduce.6.cloned.1.call-start = ((), (), s32[]{:S(2)}) async-start(), calls=%async_computation.3 | async-start | bytes 4194304 | tf_op jit(solution)/shard_map/psum | solution.py:57
  360.0 7.5 %copy-start = (bf16[2048,256]{1,0:T(8,128)(2,1)S(1)}, bf16[2048,256]{1,0:T(8,128)(2,1)}, u32[]{:S(2)}) copy-start(bf16[2048,256]{1,0:T(8,128)(2,1)} %param.11) | copy-start | bytes 3145732
  360.0 7.5 %copy-start.2 = (f32[2048]{0:T(1024)S(1)}, f32[2048]{0:T(1024)}, u32[]{:S(2)}) copy-start(f32[2048]{0:T(1024)} %param.13) | copy-start | bytes 24580
  360.0 7.5 %copy-start.5 = (f32[256]{0:T(256)S(1)}, f32[256]{0:T(256)}, u32[]{:S(2)}) copy-start(f32[256]{0:T(256)} %param.21) | copy-start | bytes 3076
  367.5 65.8 %copy-start.1 = (bf16[2048,256]{1,0:T(8,128)(2,1)S(1)}, bf16[2048,256]{1,0:T(8,128)(2,1)}, u32[]{:S(2)}) copy-start(bf16[2048,256]{1,0:T(8,128)(2,1)} %param.12) | copy-start | bytes 3145732
  433.3 65.3 %copy-start.6 = (f32[256]{0:T(256)}, f32[256]{0:T(256)S(1)}, u32[]{:S(2)}) copy-start(f32[256]{0:T(256)S(1)} %div.17) | copy-start | bytes 3076
  496.8 1.8 copy-start.7
Sparse Core Ops, SparseCore 0:
  164.0 161.3 all-reduce.5
